TPU v7x, 32 devices: a whole 2x2x4 slice. The times are simulated.
32 devices in a mesh: row: 8 (over z, core), col: 4 (over y, x).
Axes of the slice: x: 2, y: 2, z: 4, core: 2. Of those that a mesh axis runs over, the one named last changes fastest.
Arguments:
- points: bfloat16 [2048, 1024], P(('row', 'col')), may hold values from -6 to 6
- factor: float32 [2048, 256], P(('row', 'col')), may hold values from 0 to 1
Outputs:
- factor_out: float32 [2048, 256], P(('row', 'col'))
All inputs are finite; a program needn't handle non-finite values.
Results may differ from a plain program's by a relative error of at most 0.002.
The roundings to bfloat16 on the way count: a program that leaves them out, or rounds other values in their place, can miss the bound.
Values may be sent and summed in bfloat16 or wider, within the bound.
A program may use at most 64 MiB of HBM per device.

v0:
```python
import math
import jax
import jax.numpy as jnp
from jax import lax
from jax.sharding import PartitionSpec as P

EMBED_WIDTH = 1024
ITERS = 2


def shards(points, factor):
    nrow = lax.axis_size("row")
    ncol = lax.axis_size("col")
    pts = points.shape[0]
    rank = factor.shape[1]
    total = pts * nrow * ncol
    row_pts = lax.all_gather(points, "col", axis=0, tiled=True)
    col_pts = lax.all_gather(points, "row", axis=0, tiled=True)
    gram_matrix = lax.dot_general(
        row_pts, col_pts, (((1,), (1,)), ((), ())), preferred_element_type=jnp.float32
    )
    row_sq = jnp.sum(jnp.square(row_pts.astype(jnp.float32)), axis=1)
    col_sq = jnp.sum(jnp.square(col_pts.astype(jnp.float32)), axis=1)
    kern = jnp.exp((2.0 * gram_matrix - row_sq[:, None] - col_sq[None, :]) * (0.5 / EMBED_WIDTH))
    row_sum, band = lax.psum((jnp.sum(kern, axis=1), jnp.sum(kern)), "col")
    col_sum, grand = lax.psum((jnp.sum(kern, axis=0), band), "row")
    affinity = (
        kern - row_sum[:, None] / total - col_sum[None, :] / total + grand / (total * total)
    ).astype(jnp.bfloat16)
    unit = 2.0 / math.sqrt(total * rank)
    h = factor * unit
    for step in range(ITERS):
        hb = h.astype(jnp.bfloat16)
        copies = lax.all_gather(hb, "row", axis=0, tiled=True)
        ah = lax.psum_scatter(
            jnp.dot(affinity, copies, preferred_element_type=jnp.float32),
            "col",
            scatter_dimension=0,
            tiled=True,
        )
        local_gram = lax.dot_general(
            h, h, (((0,), (0,)), ((), ())), precision=lax.Precision.HIGHEST
        )
        hh = lax.psum(local_gram, ("row", "col"))
        scale = 0.5 / jnp.sqrt(jnp.sum(hh * hh) + 1e-06)
        h = jnp.maximum(h - scale * (jnp.dot(h, hh, precision=lax.Precision.HIGHEST) - ah), 0.0)
    return h / unit


def solution(mesh):
    in_specs = (P(("row", "col"), None), P(("row", "col"), None))
    out_specs = P(("row", "col"), None)
    return jax.shard_map(shards, mesh=mesh, in_specs=in_specs, out_specs=out_specs, check_vma=False)
```

profile of v0, /device:TPU:0, one launch (start us, length us, event | category | flops | bytes accessed | tf_op | source)
XLA Modules:
  0.0 301.0 jit_solution(7194826416192646812)
XLA Ops:
  7.4 0.0 copy-start.1
  7.4 0.0 all-gather.2.cloned.1.call-start
  7.4 0.7 all-gather.2.cloned.1.call-update
  8.1 0.0 all-reduce.5.cloned.1.call-start
  8.1 2.0 fusion.12
  10.2 0.0 all-reduce.5.cloned.1.call-update
  10.2 0.0 reduce-scatter.3.cloned.1.call-start
  10.3 11.9 %all_gather.12 = bf16[256,1024]{1,0:T(8,128)(2,1)S(1)} all-gather(bf16[64,1024]{1,0:T(8,128)(2,1)} %param.2), channel_id=1, replica_groups=mesh['row'=8,'col'=4] {'col'}, dimensions={0}, use_global_device_ids=true | all-gather | bytes 655360 | tf_op jit(solution)/shard_map/all_gather | solution.py:17
  22.1 0.0 copy-done.1
  22.2 0.2 multiply_reduce_fusion.1
  22.3 15.2 %all_gather.14 = bf16[512,256]{1,0:T(8,128)(2,1)S(1)} all-gather(bf16[64,256]{1,0:T(8,128)(2,1)S(1)} %multiply_convert_fusion), channel_id=1, replica_groups=mesh['row'=8,'col'=4] {'row'}, dimensions={0}, use_global_device_ids=true | all-gather | bytes 294912 | tf_op jit(solution)/shard_map/all_gather | solution.py:34
  37.6 0.0 all-gather.2.cloned.1.call-done
  37.6 0.0 copy-start
  37.6 1.6 multiply_reduce_fusion
  39.2 0.0 copy-done
  39.2 1.2 fusion.20
  40.4 9.6 %all-reduce.1 = (f32[]{:T(128)}, f32[256]{0:T(256)S(1)}) all-reduce(f32[]{:T(128)} %get-tuple-element.6, f32[256]{0:T(256)S(1)} %get-tuple-element.5), channel_id=1, replica_groups=mesh['row'=8,'col'=4] {'col'}, use_global_device_ids=true, to_apply=%region_9.0 | all-reduce | flops 257 | bytes 2056 | tf_op jit(solution)/shard_map/psum | solution.py:25
  50.0 15.4 %all-reduce = (f32[]{:T(128)}, f32[512]{0:T(512)S(1)}) all-reduce(f32[]{:T(128)} %get-tuple-element.10, f32[512]{0:T(512)S(1)} %get-tuple-element.7), channel_id=1, replica_groups=mesh['row'=8,'col'=4] {'row'}, use_global_device_ids=true, to_apply=%region_10.0 | all-reduce | flops 513 | bytes 4104 | tf_op jit(solution)/shard_map/psum | solution.py:26
  66.1 1.0 fusion.19
  67.1 0.0 reduce-scatter.3.cloned.1.call-update
  67.1 0.0 all-reduce.7.cloned.1.call-start
  67.2 78.5 %all-reduce.5.cloned.1.call-done = f32[256,256]{1,0:T(8,128)} async-done(((f32[256,256]{1,0:T(8,128)}), f32[256,256]{1,0:T(8,128)}) %all-reduce.5.cloned.1.call-update) | async-done | bytes 262160 | tf_op jit(solution)/shard_map/psum | solution.py:44
  145.6 1.6 multiply_reduce_fusion.3
  147.9 0.0 reduce-scatter.3.cloned.1.call-done
  148.0 1.2 fusion.21
  149.2 14.2 %all_gather.15 = bf16[512,256]{1,0:T(8,128)(2,1)S(1)} all-gather(bf16[64,256]{1,0:T(8,128)(2,1)S(1)} %get-tuple-element.13), channel_id=1, replica_groups=mesh['row'=8,'col'=4] {'row'}, dimensions={0}, use_global_device_ids=true | all-gather | bytes 294912 | tf_op jit(solution)/shard_map/all_gather | solution.py:34
  163.4 1.1 fusion.22
  164.5 0.0 all-reduce.7.cloned.1.call-update
  164.5 0.0 reduce-scatter.5.cloned.1.call-start
  164.6 1.0 fusion.18
  165.6 0.0 reduce-scatter.5.cloned.1.call-update
  165.6 124.1 %all-reduce.7.cloned.1.call-done = f32[256,256]{1,0:T(8,128)} async-done(((f32[256,256]{1,0:T(8,128)}), f32[256,256]{1,0:T(8,128)}) %all-reduce.7.cloned.1.call-update) | async-done | bytes 262160 | tf_op jit(solution)/shard_map/psum | solution.py:44
  289.7 1.6 multiply_reduce_fusion.2
  292.0 0.0 reduce-scatter.5.cloned.1.call-done
  292.0 1.8 fusion.7
  (3 shorter events, 0.0 us)
Async XLA Ops:
  7.4 14.8 %copy-start.1 = (f32[64,256]{1,0:T(8,128)S(1)}, f32[64,256]{1,0:T(8,128)}, u32[]{:S(2)}) copy-start(f32[64,256]{1,0:T(8,128)} %param.3) | copy-start | bytes 196612
  7.4 30.2 %all-gather.2.cloned.1.call-start = ((), (), s32[]{:S(2)}) async-start(), calls=%async_computation.3 | async-start | bytes 1179648 | tf_op jit(solution)/shard_map/all_gather | solution.py:18
  8.1 137.5 %all-reduce.5.cloned.1.call-start = ((), (), s32[]{:S(2)}) async-start(), calls=%async_computation.2 | async-start | bytes 524288 | tf_op jit(solution)/shard_map/psum | solution.py:44
  10.2 137.8 %reduce-scatter.3.cloned.1.call-start = ((), (), s32[]{:S(2)}) async-start(), calls=%async_computation.4 | async-start | bytes 327680 | tf_op jit(solution)/shard_map/reduce_scatter | solution.py:35
  37.6 1.6 copy-start
  67.1 222.6 %all-reduce.7.cloned.1.call-start = ((), (), s32[]{:S(2)}) async-start(), calls=%async_computation.5 | async-start | bytes 524288 | tf_op jit(solution)/shard_map/psum | solution.py:44
  164.5 127.5 %reduce-scatter.5.cloned.1.call-start = ((), (), s32[]{:S(2)}) async-start(), calls=%async_computation.6 | async-start | bytes 327680 | tf_op jit(solution)/shard_map/reduce_scatter | solution.py:35
Sparse Core Ops, SparseCore 0:
  9.8 26.2 all-gather.1
  67.2 21.1 reduce-scatter.2
  168.1 23.4 reduce-scatter.4
Sparse Core Ops, SparseCore 1:
  14.1 131.5 all-reduce.4
  164.6 125.0 all-reduce.6
where the time goes:
time: 301 us
  waiting for transfers between devices  203 us (67%)
  blocking collectives  66.4 us (22%)
  between operations  16.6 us (6%)
  matrix products  9.4 us (3%)
  other arithmetic  5.03 us (2%)
    psum x2, waiting for transfers between devices, shards(): hh = lax.psum(local_gram, ('row', 'col'))  203 us
    all_gather x2, blocking collectives, shards(): copies = lax.all_gather(hb, 'row', axis=0, tiled=True)  29.4 us
    psum x1, blocking collectives, shards(): col_sum, grand = lax.psum((jnp.sum(kern, axis=0), band), 'row')  15.4 us
    all_gather x1, blocking collectives, shards(): row_pts = lax.all_gather(points, 'col', axis=0, tiled=True)  11.9 us
    psum x1, blocking collectives, shards(): row_sum, band = lax.psum((jnp.sum(kern, axis=1), jnp.sum(kern)), 'col')  9.6 us
  transfers between devices with their start and end apart: 5, of which 2 were waited for; matrix products, arithmetic and copies ran while one was open for 3% of the time, Pallas kernels for 0%

commit v1 on v0

--- a/solution.py
+++ b/solution.py
@@ -41,7 +41,8 @@
         local_gram = lax.dot_general(
             h, h, (((0,), (0,)), ((), ())), precision=lax.Precision.HIGHEST
         )
-        hh = lax.psum(local_gram, ("row", "col"))
+        inner = lax.psum(local_gram, "col")
+        hh = lax.psum(inner, "row")
         scale = 0.5 / jnp.sqrt(jnp.sum(hh * hh) + 1e-06)
         h = jnp.maximum(h - scale * (jnp.dot(h, hh, precision=lax.Precision.HIGHEST) - ah), 0.0)
     return h / unit

time: 301 us -> 227 us (0.75)
  waiting for transfers between devices: 203 us -> 129 us
    psum x2 -> x4, waiting for transfers between devices: 203 us -> 128 us  [the longest x2 81 us: shards(): hh = lax.psum(inner, 'row')]
  transfers between devices with their start and end apart: 5 -> 7, of which waited for: 2 -> 4; matrix products, arithmetic and copies ran while one was open for 3% -> 4% of each run, Pallas kernels for 0% -> 0%
where the time goes in v1:
time: 227 us
  waiting for transfers between devices  129 us (57%)
  blocking collectives  66.6 us (29%)
  between operations  16.9 us (7%)
  matrix products  9.44 us (4%)
  other arithmetic  5.03 us (2%)
    psum x2, waiting for transfers between devices, shards(): hh = lax.psum(inner, 'row')  81 us
    psum x2, waiting for transfers between devices, shards(): inner = lax.psum(local_gram, 'col')  46.9 us
    all_gather x2, blocking collectives, shards(): copies = lax.all_gather(hb, 'row', axis=0, tiled=True)  29.4 us
    psum x1, blocking collectives, shards(): col_sum, grand = lax.psum((jnp.sum(kern, axis=0), band), 'row')  14.5 us
    all_gather x1, blocking collectives, shards(): row_pts = lax.all_gather(points, 'col', axis=0, tiled=True)  13.2 us
    psum x1, blocking collectives, shards(): row_sum, band = lax.psum((jnp.sum(kern, axis=1), jnp.sum(kern)), 'col')  9.53 us
  transfers between devices with their start and end apart: 7, of which 4 were waited for; matrix products, arithmetic and copies ran while one was open for 4% of the time, Pallas kernels for 0%

profile of v1, /device:TPU:0, one launch (start us, length us, event | category | flops | bytes accessed | tf_op | source)
XLA Modules:
  0.0 226.8 jit_solution(3958368545448687593)
XLA Ops:
  7.4 0.0 copy-start.1
  7.4 0.0 all-reduce.7.cloned.1.call-start
  7.4 2.1 fusion.12
  9.4 0.0 all-reduce.7.cloned.1.call-update
  9.5 0.0 all-gather.2.cloned.1.call-start
  9.5 0.5 all-gather.2.cloned.1.call-update
  10.1 0.0 all-reduce.9.cloned.1.call-start
  10.1 13.2 %all_gather.12 = bf16[256,1024]{1,0:T(8,128)(2,1)S(1)} all-gather(bf16[64,1024]{1,0:T(8,128)(2,1)} %param.2), channel_id=1, replica_groups=mesh['row'=8,'col'=4] {'col'}, dimensions={0}, use_global_device_ids=true | all-gather | bytes 655360 | tf_op jit(solution)/shard_map/all_gather | solution.py:17
  23.3 0.0 copy-done.1
  23.3 15.2 %all_gather.14 = bf16[512,256]{1,0:T(8,128)(2,1)S(1)} all-gather(bf16[64,256]{1,0:T(8,128)(2,1)S(1)} %multiply_convert_fusion), channel_id=1, replica_groups=mesh['row'=8,'col'=4] {'row'}, dimensions={0}, use_global_device_ids=true | all-gather | bytes 294912 | tf_op jit(solution)/shard_map/all_gather | solution.py:34
  38.6 0.2 multiply_reduce_fusion.1
  38.7 18.9 %all-reduce.7.cloned.1.call-done = f32[256,256]{1,0:T(8,128)} async-done(((f32[256,256]{1,0:T(8,128)}), f32[256,256]{1,0:T(8,128)}) %all-reduce.7.cloned.1.call-update) | async-done | bytes 262160 | tf_op jit(solution)/shard_map/psum | solution.py:44
  57.6 0.0 all-reduce.9.cloned.1.call-update
  57.6 0.0 reduce-scatter.3.cloned.1.call-start
  57.7 0.0 all-gather.2.cloned.1.call-done
  57.7 0.0 copy-start
  57.7 1.6 multiply_reduce_fusion
  59.3 0.0 copy-done
  59.3 1.2 fusion.20
  60.6 9.5 %all-reduce.1 = (f32[]{:T(128)}, f32[256]{0:T(256)S(1)}) all-reduce(f32[]{:T(128)} %get-tuple-element.6, f32[256]{0:T(256)S(1)} %get-tuple-element.5), channel_id=1, replica_groups=mesh['row'=8,'col'=4] {'col'}, use_global_device_ids=true, to_apply=%region_10.0 | all-reduce | flops 257 | bytes 2056 | tf_op jit(solution)/shard_map/psum | solution.py:25
  70.1 14.5 %all-reduce = (f32[]{:T(128)}, f32[512]{0:T(512)S(1)}) all-reduce(f32[]{:T(128)} %get-tuple-element.10, f32[512]{0:T(512)S(1)} %get-tuple-element.7), channel_id=1, replica_groups=mesh['row'=8,'col'=4] {'row'}, use_global_device_ids=true, to_apply=%region_11.0 | all-reduce | flops 513 | bytes 4104 | tf_op jit(solution)/shard_map/psum | solution.py:26
  85.2 1.0 fusion.19
  86.2 0.0 reduce-scatter.3.cloned.1.call-update
  86.3 0.0 all-reduce.11.cloned.1.call-start
  86.3 26.7 %all-reduce.9.cloned.1.call-done = f32[256,256]{1,0:T(8,128)} async-done(((f32[256,256]{1,0:T(8,128)}), f32[256,256]{1,0:T(8,128)}) %all-reduce.9.cloned.1.call-update) | async-done | bytes 262160 | tf_op jit(solution)/shard_map/psum | solution.py:45
  113.0 1.6 multiply_reduce_fusion.3
  115.3 0.0 reduce-scatter.3.cloned.1.call-done
  115.3 1.2 fusion.21
  116.5 1.1 fusion.22
  117.6 0.0 all-reduce.11.cloned.1.call-update
  117.7 0.0 all-reduce.13.cloned.1.call-start
  117.7 14.2 %all_gather.15 = bf16[512,256]{1,0:T(8,128)(2,1)S(1)} all-gather(bf16[64,256]{1,0:T(8,128)(2,1)S(1)} %get-tuple-element.13), channel_id=1, replica_groups=mesh['row'=8,'col'=4] {'row'}, dimensions={0}, use_global_device_ids=true | all-gather | bytes 294912 | tf_op jit(solution)/shard_map/all_gather | solution.py:34
  131.9 28.0 %all-reduce.11.cloned.1.call-done = f32[256,256]{1,0:T(8,128)} async-done(((f32[256,256]{1,0:T(8,128)}), f32[256,256]{1,0:T(8,128)}) %all-reduce.11.cloned.1.call-update) | async-done | bytes 262160 | tf_op jit(solution)/shard_map/psum | solution.py:44
  159.9 0.0 all-reduce.13.cloned.1.call-update
  159.9 0.0 reduce-scatter.5.cloned.1.call-start
  160.0 1.0 fusion.18
  161.0 0.0 reduce-scatter.5.cloned.1.call-update
  161.0 54.3 %all-reduce.13.cloned.1.call-done = f32[256,256]{1,0:T(8,128)} async-done(((f32[256,256]{1,0:T(8,128)}), f32[256,256]{1,0:T(8,128)}) %all-reduce.13.cloned.1.call-update) | async-done | bytes 262160 | tf_op jit(solution)/shard_map/psum | solution.py:45
  215.3 1.6 multiply_reduce_fusion.2
  217.6 0.0 reduce-scatter.5.cloned.1.call-done
  217.6 1.8 fusion.7
  (3 shorter events, 0.0 us)
Async XLA Ops:
  7.4 16.0 %copy-start.1 = (f32[64,256]{1,0:T(8,128)S(1)}, f32[64,256]{1,0:T(8,128)}, u32[]{:S(2)}) copy-start(f32[64,256]{1,0:T(8,128)} %param.3) | copy-start | bytes 196612
  7.4 50.3 %all-reduce.7.cloned.1.call-start = ((), (), s32[]{:S(2)}) async-start(), calls=%async_computation.2 | async-start | bytes 524288 | tf_op jit(solution)/shard_map/psum | solution.py:44
  9.5 48.2 %all-gather.2.cloned.1.call-start = ((), (), s32[]{:S(2)}) async-start(), calls=%async_computation.4 | async-start | bytes 1179648 | tf_op jit(solution)/shard_map/all_gather | solution.py:18
  10.1 102.9 %all-reduce.9.cloned.1.call-start = ((), (), s32[]{:S(2)}) async-start(), calls=%async_computation.3 | async-start | bytes 524288 | tf_op jit(solution)/shard_map/psum | solution.py:45
  57.6 57.6 %reduce-scatter.3.cloned.1.call-start = ((), (), s32[]{:S(2)}) async-start(), calls=%async_computation.5 | async-start | bytes 327680 | tf_op jit(solution)/shard_map/reduce_scatter | solution.py:35
  57.7 1.6 copy-start
  86.3 73.7 %all-reduce.11.cloned.1.call-start = ((), (), s32[]{:S(2)}) async-start(), calls=%async_computation.6 | async-start | bytes 524288 | tf_op jit(solution)/shard_map/psum | solution.py:44
  117.7 97.6 %all-reduce.13.cloned.1.call-start = ((), (), s32[]{:S(2)}) async-start(), calls=%async_computation.7 | async-start | bytes 524288 | tf_op jit(solution)/shard_map/psum | solution.py:45
  159.9 57.7 %reduce-scatter.5.cloned.1.call-start = ((), (), s32[]{:S(2)}) async-start(), calls=%async_computation.8 | async-start | bytes 327680 | tf_op jit(solution)/shard_map/reduce_scatter | solution.py:35
Sparse Core Ops, SparseCore 0:
  11.1 46.4 all-reduce.6
  86.4 21.5 reduce-scatter.2
  117.8 42.0 all-reduce.10
  163.2 24.3 reduce-scatter.4
Sparse Core Ops, SparseCore 1:
  11.6 26.0 all-gather.1
  57.7 55.2 all-reduce.8
  160.0 55.2 all-reduce.12
